TPU v7x, 32 devices: a whole 2x2x4 slice. The times are simulated.
32 devices in a mesh: req: 8 (over z, y), kvh: 2 (over x), ffn: 2 (over core).
Axes of the slice: x: 2, y: 2, z: 4, core: 2. Of those that a mesh axis runs over, the one named last changes fastest.
Arguments:
- queries: bfloat16 [8, 64, 8192], P('req', None, 'kvh'), may hold values from -8 to 8
- tree_keys: bfloat16 [8, 64, 1024], P('req', None, 'kvh'), may hold values from -4.5 to 4.5
- tree_token_values: bfloat16 [8, 64, 1024], P('req', None, 'kvh'), may hold values from -6 to 6
- cache_keys: bfloat16 [8, 8, 8192, 128], P('req', 'kvh', 'ffn'), may hold values from -4.5 to 4.5
- cached_value_rows: bfloat16 [8, 8, 8192, 128], P('req', 'kvh', 'ffn'), may hold values from -6 to 6
- lengths: int32 [8], replicated, may hold values from 1 to 8192, 16384 in all
- parents: int32 [8, 64], P('req'), may hold values from 0 to 63, as said below
- residual: float32 [512, 8192], P(('req', 'ffn'), 'kvh'), may hold values from -6 to 6
- out_weight: bfloat16 [8192, 8192], P('kvh', ('req', 'ffn')), may hold values from -0.0625 to 0.0625
- norm_gain: float32 [8192], P('kvh'), may hold values from 0.25 to 1.75
- gate_weight: bfloat16 [8192, 28672], P('kvh', ('req', 'ffn')), may hold values from -0.0625 to 0.0625
- up_weight: bfloat16 [8192, 28672], P('kvh', ('req', 'ffn')), may hold values from -0.0625 to 0.0625
- down_weight: bfloat16 [28672, 8192], P(('req', 'ffn'), 'kvh'), may hold values from -0.03125 to 0.03125
Outputs:
- layer_output: float32 [512, 8192], P(('req', 'ffn'), 'kvh')
Inputs may be any that keep to these rules, and one draw needn't show every extreme that they name: parents[r, 0] = 0, and parents[r, i] < i for every node i > 0. The lengths of all requests sum to 16384, and the largest is exactly 8192.
All inputs are finite; a program needn't handle non-finite values.
Results may differ from a plain program's by a relative error of at most 0.003.
Values may be sent and summed in bfloat16 or wider, within the bound.
A program may use at most 128 MiB of HBM per device.

v0:
```python
import jax
import jax.numpy as jnp
from jax import lax
from jax.sharding import PartitionSpec as P

D = 8192
KB = 512


MASKED = -1e30
EPSILON = 1e-05


def joined_2(array, axis, combine):
    everything = jax.tree.map(lambda part: lax.all_gather(part, axis), array)
    first = jax.tree.map(lambda part: part[0], everything)

    def hop(k, so_far):
        return combine(so_far, jax.tree.map(lambda part: part[k], everything))

    return lax.fori_loop(1, lax.axis_size(axis), hop, first)


def ancestors(parent_row, node_total):
    node_ids = jnp.arange(node_total, dtype=jnp.int32)
    upward = (parent_row[:, None] == node_ids[None, :]).astype(jnp.float32)
    reachable = jnp.minimum(jnp.eye(node_total, dtype=jnp.float32) + upward, 1.0)
    for repeat_count in range((node_total - 1).bit_length()):
        reachable = jnp.minimum(jnp.dot(reachable, reachable, precision=lax.Precision.HIGHEST), 1.0)
    return reachable > 0.5


def head_rows(query_tile_rows, head_count, head_size):
    node_total = query_tile_rows.shape[0]
    query_group_width = query_tile_rows.shape[1] // (head_count * head_size)
    shaped = query_tile_rows.reshape(node_total, head_count, query_group_width, head_size)
    return shaped.transpose(1, 2, 0, 3).reshape(
        head_count, query_group_width * node_total, head_size
    )


def absorb(running, scores, usable, value_block):
    value_sum, row_max, row_total = running
    scores = jnp.where(usable, scores, MASKED)
    highest = jnp.maximum(row_max, jnp.max(scores, axis=-1))
    weights = jnp.where(usable, jnp.exp(scores - highest[..., None]), 0.0)
    factor = jnp.exp(row_max - highest)
    row_total = row_total * factor + jnp.sum(weights, axis=-1)
    value_sum = value_sum * factor[..., None] + jnp.einsum(
        "hrk,hkd->hrd", weights, value_block.astype(jnp.float32), precision=lax.Precision.HIGHEST
    )
    return (value_sum, highest, row_total)


def combine(first, second):
    value_left, max_left, total_left = first
    value_right, max_right, total_right = second
    highest = jnp.maximum(max_left, max_right)
    factor_left = jnp.exp(max_left - highest)
    factor_right = jnp.exp(max_right - highest)
    value_sum = value_left * factor_left[..., None] + value_right * factor_right[..., None]
    return (value_sum, highest, total_left * factor_left + total_right * factor_right)


def local(
    queries,
    tree_keys,
    tree_token_values,
    cache_keys,
    cached_value_rows,
    lengths,
    parents,
    residual,
    out_weight,
    norm_gain,
    gate_weight,
    up_weight,
    down_weight,
):
    head_count = cache_keys.shape[1]
    half_len = cache_keys.shape[2]
    head_size = cache_keys.shape[3]
    node_total = queries.shape[1]
    query_group_width = queries.shape[2] // (head_count * head_size)
    row_span = query_group_width * node_total
    score_scale = head_size ** (-0.5)
    request_index = lax.axis_index("req")
    half_index = lax.axis_index("ffn")
    query_rows = head_rows(queries[0], head_count, head_size)
    fresh_state = (
        jnp.zeros((head_count, row_span, head_size), jnp.float32),
        jnp.full((head_count, row_span), MASKED, jnp.float32),
        jnp.zeros((head_count, row_span), jnp.float32),
    )
    length = lax.dynamic_index_in_dim(lengths, request_index, keepdims=False)
    live_len = jnp.clip(length - half_index * half_len, 0, half_len)
    blocks = (live_len + KB - 1) // KB
    own_keys = cache_keys[0]
    own_values = cached_value_rows[0]

    def visit(block_idx, running):
        begin_pos = block_idx * KB
        key_block = lax.dynamic_slice_in_dim(own_keys, begin_pos, KB, 1)
        value_block = lax.dynamic_slice_in_dim(own_values, begin_pos, KB, 1)
        positions = begin_pos + jnp.arange(KB, dtype=jnp.int32)
        usable = (positions < live_len)[None, None, :]
        scores = (
            jnp.einsum("hrd,hkd->hrk", query_rows, key_block, preferred_element_type=jnp.float32)
            * score_scale
        )
        return absorb(running, scores, usable, value_block)

    running = lax.fori_loop(0, blocks, visit, fresh_state)
    tree_mask = jnp.tile(ancestors(parents[0], node_total), (query_group_width, 1))
    tree_usable = jnp.logical_and(tree_mask, half_index == 0)[None]
    tree_key_rows = tree_keys[0].reshape(node_total, head_count, head_size).transpose(1, 0, 2)
    tree_value_block = (
        tree_token_values[0].reshape(node_total, head_count, head_size).transpose(1, 0, 2)
    )
    tree_score_matrix = (
        jnp.einsum("hrd,hkd->hrk", query_rows, tree_key_rows, preferred_element_type=jnp.float32)
        * score_scale
    )
    running = absorb(running, tree_score_matrix, tree_usable, tree_value_block)
    value_sum, row_max, row_total = joined_2(running, "ffn", combine)
    attention = (value_sum / row_total[..., None]).astype(jnp.bfloat16)
    attention = (
        attention.reshape(head_count, query_group_width, node_total, head_size)
        .transpose(2, 0, 1, 3)
        .reshape(node_total, head_count * query_group_width * head_size)
    )
    partial_rows = jnp.dot(
        lax.all_gather(attention, "req", axis=0, tiled=True),
        out_weight,
        preferred_element_type=jnp.float32,
    )
    regrouped = lax.all_to_all(
        partial_rows, ("req", "ffn"), split_axis=0, concat_axis=1, tiled=True
    )
    projected = lax.psum_scatter(regrouped, "kvh", scatter_dimension=1, tiled=True)
    state = residual + projected
    squares = lax.psum(jnp.sum(state * state, axis=1), "kvh")
    normed = (state * lax.rsqrt(squares / D + EPSILON)[:, None] * norm_gain).astype(jnp.bfloat16)
    block_rows = lax.all_gather(normed, ("req", "ffn"), axis=0, tiled=True)
    gate_part = jnp.dot(block_rows, gate_weight, preferred_element_type=jnp.float32)
    up_part = jnp.dot(block_rows, up_weight, preferred_element_type=jnp.float32)
    joined = jnp.concatenate([gate_part, up_part], axis=1)
    ffn_width = gate_weight.shape[1]
    shares = lax.psum_scatter(joined, "kvh", scatter_dimension=0, tiled=True)
    activated = (jax.nn.silu(shares[:, :ffn_width]) * shares[:, ffn_width:]).astype(jnp.bfloat16)
    activation = lax.all_gather(activated, "kvh", axis=0, tiled=True)
    result = lax.psum_scatter(
        jnp.dot(activation, down_weight, preferred_element_type=jnp.float32),
        ("req", "ffn"),
        scatter_dimension=0,
        tiled=True,
    )
    return state + result


def solution(mesh):
    in_specs = (
        P("req", None, "kvh"),
        P("req", None, "kvh"),
        P("req", None, "kvh"),
        P("req", "kvh", "ffn", None),
        P("req", "kvh", "ffn", None),
        P(),
        P("req", None),
        P(("req", "ffn"), "kvh"),
        P("kvh", ("req", "ffn")),
        P("kvh"),
        P("kvh", ("req", "ffn")),
        P("kvh", ("req", "ffn")),
        P(("req", "ffn"), "kvh"),
    )
    out_specs = P(("req", "ffn"), "kvh")
    return jax.shard_map(local, mesh=mesh, in_specs=in_specs, out_specs=out_specs, check_vma=False)
```

profile of v0, /device:TPU:0, one launch (start us, length us, event | category | flops | bytes accessed | tf_op | source)
XLA Modules:
  0.0 563.1 jit_solution(8850163666659074797)
XLA Ops:
  6.5 1.2 dynamic_slice.22
  12.2 1.1 copy.44
  13.7 25.4 %while.2 = (s32[]{:T(128)}, f32[4,512,128]{2,1,0:T(8,128)S(1)}, f32[4,512]{1,0:T(4,128)S(1)}, f32[4,512]{1,0:T(4,128)S(1)}, s32[]{:T(128)}, /*index=5*/s32[]{:T(...) while((s32[]{:T(128)}, f32[4,512,128]{2,1,0:T(8,128)S(1)}, ...), condition=%wide.region_3.4_spmd, body=%wide.region_0.3_spmd.sunk | while | flops 1892160512 | bytes 16386747 | solution.py:113
  13.7 1.8 bitcast_reduce_fusion.2
  15.5 1.1 fusion.85
  16.7 5.5 fusion.86
  22.2 1.8 bitcast_reduce_fusion.2
  25.2 5.5 fusion.86
  30.7 1.8 bitcast_reduce_fusion.2
  33.6 5.5 fusion.86
  39.6 2.2 convolution_add_fusion
  41.9 1.8 all-gather.4
  43.8 1.8 all-gather.3
  46.2 50.5 %all-gather.16.cloned.1.call-done = f32[8,512,128]{2,1,0:T(8,128)} async-done(((f32[4,512,128]{2,1,0:T(8,128)}), f32[8,512,128]{2,1,0:T(8,128)}) %all-gather.16.cloned.1.call-update) | async-done | bytes 2097168 | tf_op jit(solution)/shard_map/all_gather | solution.py:15
  96.7 1.7 fusion.49
  98.4 2.4 fusion.28
  102.0 73.9 %all-gather.10.cloned.1.call-done = bf16[512,4096]{1,0:T(8,128)(2,1)} async-done(((bf16[64,4096]{1,0:T(8,128)(2,1)}), bf16[512,4096]{1,0:T(8,128)(2,1)}) %all-gather.10.cloned.1.call-update) | async-done | bytes 4194320 | tf_op jit(solution)/shard_map/all_gather | solution.py:133
  175.9 5.8 %fusion.53 = f32[512,512]{1,0:T(8,128)S(1)} fusion(bf16[512,4096]{1,0:T(8,128)(2,1)} %all-gather.10.cloned.1.call-done, bf16[4096,512]{1,0:T(8,128)(2,1)} %param.23), kind=kOutput, calls=%fused_computation.78 | convolution fusion | flops 2147483648 | bytes 9437184 | tf_op jit(solution)/shard_map/dot_general | solution.py:132
  181.7 27.9 %all_to_all.19 = f32[16,32,512]{2,1,0:T(8,128)S(1)} all-to-all(f32[16,32,512]{2,1,0:T(8,128)S(1)} %bitcast.85), channel_id=1, replica_groups=mesh['req'=8,'kvh'=2,'ffn'=2] {'req','ffn'}, dimensions={0} | all-to-all | bytes 2097152 | tf_op jit(solution)/shard_map/all_to_all | solution.py:137
  210.7 20.8 %reduce-scatter.4.cloned.1.call-done = f32[32,4096]{1,0:T(8,128)} async-done(((f32[32,8192]{1,0:T(8,128)}), f32[32,4096]{1,0:T(8,128)}) %reduce-scatter.4.cloned.1.call-update) | async-done | bytes 524304 | tf_op jit(solution)/shard_map/reduce_scatter | solution.py:140
  231.6 1.2 multiply_reduce_fusion
  232.8 4.9 psum.7
  238.6 50.5 %all-gather.12.cloned.1.call-done = bf16[512,4096]{1,0:T(8,128)(2,1)} async-done(((bf16[32,4096]{1,0:T(8,128)(2,1)}), bf16[512,4096]{1,0:T(8,128)(2,1)}) %all-gather.12.cloned.1.call-update) | async-done | bytes 4194320 | tf_op jit(solution)/shard_map/all_gather | solution.py:144
  289.1 11.8 %fusion.55 = f32[512,1792]{1,0:T(8,128)S(1)} fusion(bf16[512,4096]{1,0:T(8,128)(2,1)} %all-gather.12.cloned.1.call-done, bf16[4096,1792]{1,0:T(8,128)(2,1)} %param.26), kind=kOutput, calls=%fused_computation.80 | convolution fusion | flops 7516192768 | bytes 22544384 | tf_op jit(solution)/shard_map/dot_general | solution.py:146
  301.0 11.1 %fusion.54 = f32[512,1792]{1,0:T(8,128)S(1)} fusion(bf16[512,4096]{1,0:T(8,128)(2,1)S(1)} %copy-done.2, bf16[4096,1792]{1,0:T(8,128)(2,1)} %param.25), kind=kOutput, calls=%fused_computation.79 | convolution fusion | flops 7516192768 | bytes 22544384 | tf_op jit(solution)/shard_map/dot_general | solution.py:145
  312.1 4.0 pad_maximum_fusion
  316.2 87.1 %reduce-scatter.6.cloned.1.call-done = f32[256,3584]{1,0:T(8,128)} async-done(((f32[512,3584]{1,0:T(8,128)}), f32[256,3584]{1,0:T(8,128)}) %reduce-scatter.6.cloned.1.call-update) | async-done | bytes 3670032 | tf_op jit(solution)/shard_map/reduce_scatter | solution.py:149
  403.4 3.5 fusion.22
  406.9 30.2 %all-gather.14.cloned.1.call-done = bf16[512,1792]{1,0:T(8,128)(2,1)} async-done(((bf16[256,1792]{1,0:T(8,128)(2,1)}), bf16[512,1792]{1,0:T(8,128)(2,1)}) %all-gather.14.cloned.1.call-update) | async-done | bytes 1835024 | tf_op jit(solution)/shard_map/all_gather | solution.py:151
  437.2 13.6 %fusion.56 = f32[512,4096]{1,0:T(8,128)} fusion(bf16[512,1792]{1,0:T(8,128)(2,1)} %all-gather.14.cloned.1.call-done, bf16[1792,4096]{1,0:T(8,128)(2,1)} %param.27), kind=kOutput, calls=%fused_computation.81 | convolution fusion | flops 7516192768 | bytes 24903680 | tf_op jit(solution)/shard_map/dot_general | solution.py:153
  450.8 103.6 %reduce-scatter.8.cloned.1.call-done = f32[32,4096]{1,0:T(8,128)} async-done(((f32[512,4096]{1,0:T(8,128)}), f32[32,4096]{1,0:T(8,128)}) %reduce-scatter.8.cloned.1.call-update) | async-done | bytes 524304 | tf_op jit(solution)/shard_map/reduce_scatter | solution.py:152
  554.4 1.9 add.96
  (67 shorter events, 11.0 us)
Async XLA Ops:
  6.5 90.2 %all-gather.16.cloned.1.call-start = ((), (), s32[]{:S(2)}) async-start(), calls=%async_computation.10 | async-start | bytes 3145728 | tf_op jit(solution)/shard_map/all_gather | solution.py:15
  41.8 134.1 %all-gather.10.cloned.1.call-start = ((), (), s32[]{:S(2)}) async-start(), calls=%async_computation.4 | async-start | bytes 4718592 | tf_op jit(solution)/shard_map/all_gather | solution.py:133
  101.8 129.8 %reduce-scatter.4.cloned.1.call-start = ((), (), s32[]{:S(2)}) async-start(), calls=%async_computation.5 | async-start | bytes 1572864 | tf_op jit(solution)/shard_map/reduce_scatter | solution.py:140
  181.7 49.9 %copy-start = (f32[32,4096]{1,0:T(8,128)S(1)}, f32[32,4096]{1,0:T(8,128)}, u32[]{:S(2)}) copy-start(f32[32,4096]{1,0:T(8,128)} %param.22) | copy-start | bytes 1572868
  181.7 56.0 %copy-start.1 = (f32[4096]{0:T(1024)S(1)}, f32[4096]{0:T(1024)}, u32[]{:S(2)}) copy-start(f32[4096]{0:T(1024)} %param.24) | copy-start | bytes 49156
  210.7 78.4 %all-gather.12.cloned.1.call-start = ((), (), s32[]{:S(2)}) async-start(), calls=%async_computation.6 | async-start | bytes 4456448 | tf_op jit(solution)/shard_map/all_gather | solution.py:144
  238.6 164.8 %reduce-scatter.6.cloned.1.call-start = ((), (), s32[]{:S(2)}) async-start(), calls=%async_computation.7 | async-start | bytes 11010048 | tf_op jit(solution)/shard_map/reduce_scatter | solution.py:149
  289.1 11.9 %copy-start.2 = (bf16[512,4096]{1,0:T(8,128)(2,1)S(1)}, bf16[512,4096]{1,0:T(8,128)(2,1)}, u32[]{:S(2)}) copy-start(bf16[512,4096]{1,0:T(8,128)(2,1)} %all-gather.12.cloned.1.call-done) | copy-start | bytes 12582916
  316.2 121.0 %all-gather.14.cloned.1.call-start = ((), (), s32[]{:S(2)}) async-start(), calls=%async_computation.8 | async-start | bytes 2752512 | tf_op jit(solution)/shard_map/all_gather | solution.py:151
  406.9 147.5 %reduce-scatter.8.cloned.1.call-start = ((), (), s32[]{:S(2)}) async-start(), calls=%async_computation.9 | async-start | bytes 8912896 | tf_op jit(solution)/shard_map/reduce_scatter | solution.py:152
Sparse Core Ops, SparseCore 0:
  41.9 54.7 all-gather.15
  101.9 73.9 all-gather.9
  210.8 20.7 reduce-scatter.3
  238.7 50.3 all-gather.11
  316.3 87.0 reduce-scatter.5
  407.0 30.1 all-gather.13
  450.9 103.4 reduce-scatter.7
where the time goes:
time: 563 us
  waiting for transfers between devices  417 us (74%)
  matrix products  68.4 us (12%)
  blocking collectives  36.4 us (6%)
  other arithmetic  17.4 us (3%)
  between operations  14.3 us (3%)
  local copies, waits for them, and re-layouts  9.07 us (2%)
    reduce_scatter x1, waiting for transfers between devices, local(): lax.psum_scatter(jnp.dot(activation, down_weight, preferred_element_type=...  104 us
    reduce_scatter x1, waiting for transfers between devices, local(): shares = lax.psum_scatter(joined, 'kvh', scatter_dimension=0, tiled=True)  87.1 us
    all_gather x1, waiting for transfers between devices, local(): lax.all_gather(attention, 'req', axis=0, tiled=True)  73.9 us
    all_gather x1, waiting for transfers between devices, joined_2(): everything = jax.tree.map(lambda part: lax.all_gather(part, axis), array)  50.5 us
    all_gather x1, waiting for transfers between devices, local(): block_rows = lax.all_gather(normed, ('req', 'ffn'), axis=0, tiled=True)  50.5 us
    all_gather x1, waiting for transfers between devices, local(): activation = lax.all_gather(activated, 'kvh', axis=0, tiled=True)  30.2 us
    all_to_all x1, blocking collectives, local(): lax.all_to_all(partial_rows, ('req', 'ffn'), split_axis=0, concat_axis=1,...  27.9 us
    reduce_scatter x1, waiting for transfers between devices, local(): lax.psum_scatter(regrouped, 'kvh', scatter_dimension=1, tiled=True)  20.8 us
  transfers between devices with their start and end apart: 7, of which 7 were waited for; matrix products, arithmetic and copies ran while one was open for 0% of the time, Pallas kernels for 0%

commit v1 on v0

v1 whole, which is shorter than its diff:
```python
import functools
import math

import jax
import jax.numpy as jnp
from jax import lax
from jax.experimental import pallas as pl
from jax.experimental.pallas import tpu as pltpu
from jax.sharding import PartitionSpec as P

MASKED = -1e30
EPSILON = 1e-05


def attend(len_ref, q_ref, tk_ref, tv_ref, k_ref, v_ref, par_ref, o_ref, ml_ref, acc, stat, *, chunk, factor):
    live = len_ref[0]
    tree_live = len_ref[1]
    nodes = q_ref.shape[0]
    size = k_ref.shape[-1]
    group = q_ref.shape[1] // size
    rows = nodes * group
    q = jnp.concatenate([q_ref[:, g * size : (g + 1) * size] for g in range(group)], axis=0)
    acc[...] = jnp.zeros_like(acc)
    stat[0:1, :] = jnp.full((1, rows), MASKED, jnp.float32)
    stat[1:2, :] = jnp.zeros((1, rows), jnp.float32)

    def scores_of(keys):
        return lax.dot_general(keys, q, (((1,), (1,)), ((), ())), preferred_element_type=jnp.float32)

    def absorb(scores, usable, values):
        if usable is not None:
            scores = jnp.where(usable, scores, MASKED)
        old = stat[0:1, :]
        top = jnp.maximum(old, jnp.max(scores, axis=0, keepdims=True))
        weights = jnp.exp2(scores * factor - top * factor)
        if usable is not None:
            weights = jnp.where(usable, weights, 0.0)
        shrink = jnp.exp2((old - top) * factor)
        stat[0:1, :] = top
        stat[1:2, :] = stat[1:2, :] * shrink + jnp.sum(weights, axis=0, keepdims=True)
        acc[...] = acc[...] * shrink + lax.dot_general(
            values, weights.astype(jnp.bfloat16), (((0,), (0,)), ((), ())), preferred_element_type=jnp.float32
        )

    full = live // chunk

    def visit(c, carry):
        at = pl.ds(pl.multiple_of(c * chunk, chunk), chunk)
        absorb(scores_of(k_ref[0, at, :]), None, v_ref[0, at, :])
        return carry

    lax.fori_loop(0, full, visit, 0)

    @pl.when(live > full * chunk)
    def _():
        at = pl.ds(pl.multiple_of(full * chunk, chunk), chunk)
        spot = full * chunk + lax.broadcasted_iota(jnp.int32, (chunk, rows), 0)
        absorb(scores_of(k_ref[0, at, :]), spot < live, v_ref[0, at, :])

    @pl.when(tree_live > 0)
    def _():
        up = lax.broadcasted_iota(jnp.int32, (nodes, nodes), 0)
        across = lax.broadcasted_iota(jnp.int32, (nodes, nodes), 1)
        link = jnp.where(up == par_ref[...], 1.0, 0.0) + jnp.where(up == across, 1.0, 0.0)
        reach = jnp.minimum(link, 1.0)
        for _ in range((nodes - 1).bit_length()):
            half = reach.astype(jnp.bfloat16)
            reach = jnp.minimum(jnp.dot(half, half, preferred_element_type=jnp.float32), 1.0)
        row = lax.broadcasted_iota(jnp.int32, (nodes, rows), 0)
        col = lax.broadcasted_iota(jnp.int32, (nodes, rows), 1)
        spread = jnp.where(lax.rem(col, nodes) == row, 1.0, 0.0).astype(jnp.bfloat16)
        mask = jnp.dot(reach.astype(jnp.bfloat16), spread, preferred_element_type=jnp.float32)
        absorb(scores_of(tk_ref[...]), mask > 0.5, tv_ref[...])

    total = stat[1:2, :]
    out = (acc[...] / jnp.where(total > 0.0, total, 1.0)).T.astype(jnp.bfloat16)
    for g in range(group):
        o_ref[:, g * size : (g + 1) * size] = out[g * nodes : (g + 1) * nodes, :]
    ml_ref[0] = jnp.concatenate([stat[0:1, :] * (size**-0.5), total], axis=0)


def attention_part(queries, tree_keys, tree_values, keys, values, lengths2, parents):
    heads, span, size = keys.shape
    nodes, width = queries.shape
    wide = width // heads
    rows = wide // size * nodes
    chunk = math.gcd(span, 1024)
    body = functools.partial(attend, chunk=chunk, factor=size**-0.5 * math.log2(math.e))
    return pl.pallas_call(
        body,
        out_shape=(
            jax.ShapeDtypeStruct((nodes, width), jnp.bfloat16),
            jax.ShapeDtypeStruct((heads, 2, rows), jnp.float32),
        ),
        grid_spec=pltpu.PrefetchScalarGridSpec(
            num_scalar_prefetch=1,
            grid=(heads,),
            in_specs=[
                pl.BlockSpec((nodes, wide), lambda h, n: (0, h)),
                pl.BlockSpec((nodes, size), lambda h, n: (0, h)),
                pl.BlockSpec((nodes, size), lambda h, n: (0, h)),
                pl.BlockSpec((1, span, size), lambda h, n: (h, 0, 0)),
                pl.BlockSpec((1, span, size), lambda h, n: (h, 0, 0)),
                pl.BlockSpec((1, nodes), lambda h, n: (0, 0)),
            ],
            out_specs=(
                pl.BlockSpec((nodes, wide), lambda h, n: (0, h)),
                pl.BlockSpec((1, 2, rows), lambda h, n: (h, 0, 0)),
            ),
            scratch_shapes=[
                pltpu.VMEM((size, rows), jnp.float32),
                pltpu.VMEM((8, rows), jnp.float32),
            ],
        ),
        compiler_params=pltpu.CompilerParams(dimension_semantics=("arbitrary",)),
    )(lengths2, queries, tree_keys, tree_values, keys, values, parents)


MESH = pl.DeviceIdType.MESH
VMEM_LIMIT = 60 * 1024 * 1024


def split_count(n):
    lo = math.isqrt(n)
    while n % lo:
        lo -= 1
    return n // lo, lo


def ring_peers(n, me):
    return [lax.rem(me + d, n) for d in range(1, n)]


def staged_places(hi_n, lo_n, core_n):
    req = lax.axis_index("req")
    hi, lo, core = req // lo_n, lax.rem(req, lo_n), lax.axis_index("ffn")
    hi_peers = [(h, {"req": h * lo_n + lo}) for h in ring_peers(hi_n, hi)]
    lo_peers = [(b, {"req": hi * lo_n + b}) for b in ring_peers(lo_n, lo)]
    core_peers = [(c, {"ffn": c}) for c in ring_peers(core_n, core)]
    return hi, lo, core, hi_peers, lo_peers, core_peers


def meet(peers):
    barrier = pltpu.get_barrier_semaphore()
    for _, where in peers:
        pl.semaphore_signal(barrier, inc=1, device_id=where, device_id_type=MESH)
    pl.semaphore_wait(barrier, len(peers))


def remote(src, dst, send, recv, where):
    return pltpu.make_async_remote_copy(
        src_ref=src, dst_ref=dst, send_sem=send, recv_sem=recv, device_id=where, device_id_type=MESH
    )


def gather_body(x_ref, out_ref, send, recv, own_sem, *, dims, pieces):
    hi_n, lo_n, core_n = dims
    hi, lo, core, hi_peers, lo_peers, core_peers = staged_places(*dims)
    wide = x_ref.shape[1] // pieces
    meet(hi_peers + lo_peers + core_peers)
    own = pltpu.make_async_copy(x_ref, out_ref.at[hi, lo, core], own_sem)
    own.start()
    first, second, third = [], [], []
    for p in range(pieces):
        cols = pl.ds(p * wide, wide)
        group = []
        for d, (_, where) in enumerate(hi_peers):
            copy = remote(
                x_ref.at[:, cols], out_ref.at[hi, lo, core, :, cols], send.at[p, d], recv.at[p, d], where
            )
            copy.start()
            group.append(copy)
        first.append(group)
    own.wait()
    base = len(hi_peers)
    for step in range(pieces + 1):
        if step < pieces:
            cols = pl.ds(step * wide, wide)
            for copy in first[step]:
                copy.wait_recv()
            group = []
            for d, (_, where) in enumerate(lo_peers):
                part = out_ref.at[:, lo, core, :, cols]
                copy = remote(part, part, send.at[step, base + d], recv.at[step, base + d], where)
                copy.start()
                group.append(copy)
            second.append(group)
        if step > 0:
            p = step - 1
            cols = pl.ds(p * wide, wide)
            for copy in second[p]:
                copy.wait_recv()
            group = []
            for d, (_, where) in enumerate(core_peers):
                at = base + len(lo_peers) + d
                part = out_ref.at[:, :, core, :, cols]
                copy = remote(part, part, send.at[p, at], recv.at[p, at], where)
                copy.start()
                group.append(copy)
            third.append(group)
    for group in third:
        for copy in group:
            copy.wait_recv()
    for group in first + second + third:
        for copy in group:
            copy.wait_send()


def gather_tokens(x, collective_id):
    dims = (*split_count(lax.axis_size("req")), lax.axis_size("ffn"))
    rows, width = x.shape
    pieces = math.gcd(width // 128, 4)
    links = sum(dims) - 3
    vmem = pl.BlockSpec(memory_space=pltpu.VMEM)
    out = pl.pallas_call(
        functools.partial(gather_body, dims=dims, pieces=pieces),
        out_shape=jax.ShapeDtypeStruct((*dims, rows, width), x.dtype),
        in_specs=[vmem],
        out_specs=vmem,
        scratch_shapes=[
            pltpu.SemaphoreType.DMA((pieces, links)),
            pltpu.SemaphoreType.DMA((pieces, links)),
            pltpu.SemaphoreType.DMA,
        ],
        compiler_params=pltpu.CompilerParams(
            collective_id=collective_id, has_side_effects=True, vmem_limit_bytes=VMEM_LIMIT
        ),
    )(x)
    return out.reshape(math.prod(dims) * rows, width)


def scatter_body(x_ref, state_ref, out_ref, got_core, mid, own_mid, got_lo, low, own_low, got_hi, send, recv, *, dims, pieces):
    hi, lo, core, hi_peers, lo_peers, core_peers = staged_places(*dims)
    hi_n, lo_n, core_n = dims
    wide = x_ref.shape[-1] // pieces
    meet(hi_peers + lo_peers + core_peers)
    first, second, third = [], [], []
    for p in range(pieces):
        cols = pl.ds(p * wide, wide)
        group = []
        for d, (c, where) in enumerate(core_peers):
            copy = remote(
                x_ref.at[:, :, c, :, cols], got_core.at[d, :, :, :, cols], send.at[p, d], recv.at[p, d], where
            )
            copy.start()
            group.append(copy)
        first.append(group)
    base_lo = len(core_peers)
    base_hi = base_lo + len(lo_peers)
    for step in range(pieces + 2):
        if step < pieces:
            p = step
            cols = pl.ds(p * wide, wide)
            for copy in first[p]:
                copy.wait_recv()

            def add_core(h, carry):
                for b in range(lo_n):
                    total = x_ref[h, b, core, :, cols]
                    for d in range(core_n - 1):
                        total = total + got_core[d, h, b, :, cols]
                    mid[h, b, :, cols] = total.astype(jnp.bfloat16)
                    own_mid[h, b, :, cols] = total
                return carry

            lax.fori_loop(0, hi_n, add_core, 0)
            group = []
            for d, (b, where) in enumerate(lo_peers):
                at = base_lo + d
                copy = remote(mid.at[:, b, :, cols], got_lo.at[d, :, :, cols], send.at[p, at], recv.at[p, at], where)
                copy.start()
                group.append(copy)
            second.append(group)
        if 1 <= step <= pieces:
            p = step - 1
            cols = pl.ds(p * wide, wide)
            for copy in second[p]:
                copy.wait_recv()

            def add_lo(h, carry):
                total = own_mid[h, lo, :, cols]
                for d in range(lo_n - 1):
                    total = total + got_lo[d, h, :, cols].astype(jnp.float32)
                low[h, :, cols] = total.astype(jnp.bfloat16)
                own_low[h, :, cols] = total
                return carry

            lax.fori_loop(0, hi_n, add_lo, 0)
            group = []
            for d, (h, where) in enumerate(hi_peers):
                at = base_hi + d
                copy = remote(low.at[h, :, cols], got_hi.at[d, :, cols], send.at[p, at], recv.at[p, at], where)
                copy.start()
                group.append(copy)
            third.append(group)
        if step >= 2:
            p = step - 2
            cols = pl.ds(p * wide, wide)
            for copy in third[p]:
                copy.wait_recv()
            total = own_low[hi, :, cols]
            for d in range(hi_n - 1):
                total = total + got_hi[d, :, cols].astype(jnp.float32)
            out_ref[:, cols] = state_ref[:, cols] + total
    for group in first + second + third:
        for copy in group:
            copy.wait_send()


def scatter_tokens(x, state, collective_id):
    dims = (*split_count(lax.axis_size("req")), lax.axis_size("ffn"))
    hi_n, lo_n, core_n = dims
    rows, width = state.shape
    pieces = math.gcd(width // 128, 4)
    links = sum(dims) - 3
    vmem = pl.BlockSpec(memory_space=pltpu.VMEM)
    return pl.pallas_call(
        functools.partial(scatter_body, dims=dims, pieces=pieces),
        out_shape=jax.ShapeDtypeStruct(state.shape, jnp.float32),
        in_specs=[vmem, vmem],
        out_specs=vmem,
        scratch_shapes=[
            pltpu.VMEM((core_n - 1, hi_n, lo_n, rows, width), jnp.float32),
            pltpu.VMEM((hi_n, lo_n, rows, width), jnp.bfloat16),
            pltpu.VMEM((hi_n, lo_n, rows, width), jnp.float32),
            pltpu.VMEM((lo_n - 1, hi_n, rows, width), jnp.bfloat16),
            pltpu.VMEM((hi_n, rows, width), jnp.bfloat16),
            pltpu.VMEM((hi_n, rows, width), jnp.float32),
            pltpu.VMEM((hi_n - 1, rows, width), jnp.bfloat16),
            pltpu.SemaphoreType.DMA((pieces, links)),
            pltpu.SemaphoreType.DMA((pieces, links)),
        ],
        compiler_params=pltpu.CompilerParams(
            collective_id=collective_id, has_side_effects=True, vmem_limit_bytes=VMEM_LIMIT
        ),
    )(x.reshape(*dims, rows, width), state)


def gated_body(gate_ref, up_ref, own_gate_ref, own_up_ref, out_ref, got_gate, got_up, send, recv, *, pieces):
    n = gate_ref.shape[0]
    rows = gate_ref.shape[1]
    me = lax.axis_index("kvh")
    peers = [(k, {"kvh": k}) for k in ring_peers(n, me)]
    wide = gate_ref.shape[2] // pieces
    meet(peers)
    first, second = [], []
    for p in range(pieces):
        cols = pl.ds(p * wide, wide)
        group = []
        for d, (k, where) in enumerate(peers):
            for half, (src, dst) in enumerate(((gate_ref, got_gate), (up_ref, got_up))):
                copy = remote(
                    src.at[k, :, cols], dst.at[d, :, cols], send.at[half, p, d], recv.at[half, p, d], where
                )
                copy.start()
                group.append(copy)
        first.append(group)
    for p in range(pieces):
        cols = pl.ds(p * wide, wide)
        for copy in first[p]:
            copy.wait_recv()
        step = math.gcd(rows, 64)

        def activate(r, carry):
            at = pl.ds(pl.multiple_of(r * step, step), step)
            gate = own_gate_ref[at, cols]
            up = own_up_ref[at, cols]
            for d in range(n - 1):
                gate = gate + got_gate[d, at, cols].astype(jnp.float32)
                up = up + got_up[d, at, cols].astype(jnp.float32)
            out_ref[me, at, cols] = (gate / (1.0 + jnp.exp(-gate)) * up).astype(jnp.bfloat16)
            return carry

        lax.fori_loop(0, rows // step, activate, 0)
        group = []
        for d, (_, where) in enumerate(peers):
            part = out_ref.at[me, :, cols]
            copy = remote(part, part, send.at[2, p, d], recv.at[2, p, d], where)
            copy.start()
            group.append(copy)
        second.append(group)
    for group in second:
        for copy in group:
            copy.wait_recv()
    for group in first + second:
        for copy in group:
            copy.wait_send()


def gated(gate, up, collective_id):
    n = lax.axis_size("kvh")
    tokens, width = gate.shape
    rows = tokens // n
    pieces = math.gcd(width // 128, 7)
    gate, up = gate.reshape(n, rows, width), up.reshape(n, rows, width)
    me = lax.axis_index("kvh")
    own_gate = lax.dynamic_index_in_dim(gate, me, keepdims=False)
    own_up = lax.dynamic_index_in_dim(up, me, keepdims=False)
    vmem = pl.BlockSpec(memory_space=pltpu.VMEM)
    out = pl.pallas_call(
        functools.partial(gated_body, pieces=pieces),
        out_shape=jax.ShapeDtypeStruct((n, rows, width), jnp.bfloat16),
        in_specs=[vmem] * 4,
        out_specs=vmem,
        scratch_shapes=[
            pltpu.VMEM((n - 1, rows, width), jnp.bfloat16),
            pltpu.VMEM((n - 1, rows, width), jnp.bfloat16),
            pltpu.SemaphoreType.DMA((3, pieces, n - 1)),
            pltpu.SemaphoreType.DMA((3, pieces, n - 1)),
        ],
        compiler_params=pltpu.CompilerParams(
            collective_id=collective_id, has_side_effects=True, vmem_limit_bytes=VMEM_LIMIT
        ),
    )(gate.astype(jnp.bfloat16), up.astype(jnp.bfloat16), own_gate, own_up)
    return out.reshape(tokens, width)


def local(
    queries,
    tree_keys,
    tree_token_values,
    cache_keys,
    cached_value_rows,
    lengths,
    parents,
    residual,
    out_weight,
    norm_gain,
    gate_weight,
    up_weight,
    down_weight,
):
    heads, half_len, size = cache_keys.shape[1:]
    nodes = queries.shape[1]
    group = queries.shape[2] // (heads * size)
    request_index = lax.axis_index("req")
    half_index = lax.axis_index("ffn")
    halves = lax.axis_size("ffn")
    features = norm_gain.shape[0] * lax.axis_size("kvh")
    length = lax.dynamic_index_in_dim(lengths, request_index, keepdims=False)
    live_len = jnp.clip(length - half_index * half_len, 0, half_len)
    lengths2 = jnp.stack([live_len, (half_index == 0).astype(jnp.int32)])
    own, ml = attention_part(
        queries[0], tree_keys[0], tree_token_values[0], cache_keys[0], cached_value_rows[0], lengths2, parents
    )
    mine_rows = nodes // halves
    pair = lax.all_to_all(own, "ffn", split_axis=0, concat_axis=0, tiled=True).reshape(halves, mine_rows, -1)
    ml_pair = lax.all_gather(ml, "ffn")
    weights = ml_pair[:, :, 1] * jnp.exp(ml_pair[:, :, 0] - jnp.max(ml_pair[:, :, 0], axis=0))
    share = (weights / jnp.sum(weights, axis=0)).reshape(halves, heads * group, nodes)
    share = lax.dynamic_slice_in_dim(share, half_index * mine_rows, mine_rows, 2).transpose(0, 2, 1)[..., None]
    mixed = jnp.sum(pair.astype(jnp.float32).reshape(halves, mine_rows, heads * group, size) * share, axis=0)
    attention = mixed.astype(jnp.bfloat16).reshape(mine_rows, heads * group * size)
    partial_rows = jnp.dot(gather_tokens(attention, 1), out_weight, preferred_element_type=jnp.float32)
    regrouped = lax.all_to_all(
        partial_rows, ("req", "ffn"), split_axis=0, concat_axis=1, tiled=True
    )
    shares = lax.all_to_all(regrouped, "kvh", split_axis=1, concat_axis=0, tiled=True)
    projected = jnp.sum(shares.reshape(-1, *residual.shape), axis=0)
    state = residual + projected
    squares = lax.psum(jnp.sum(state * state, axis=1), "kvh")
    normed = (state * lax.rsqrt(squares / features + EPSILON)[:, None] * norm_gain).astype(jnp.bfloat16)
    block_rows = gather_tokens(normed, 2)
    gate_part = jnp.dot(block_rows, gate_weight, preferred_element_type=jnp.float32)
    up_part = jnp.dot(block_rows, up_weight, preferred_element_type=jnp.float32)
    activation = gated(gate_part, up_part, 3)
    down_part = jnp.dot(activation, down_weight, preferred_element_type=jnp.float32)
    return scatter_tokens(down_part, state, 4)


def solution(mesh):
    in_specs = (
        P("req", None, "kvh"),
        P("req", None, "kvh"),
        P("req", None, "kvh"),
        P("req", "kvh", "ffn", None),
        P("req", "kvh", "ffn", None),
        P(),
        P("req", None),
        P(("req", "ffn"), "kvh"),
        P("kvh", ("req", "ffn")),
        P("kvh"),
        P("kvh", ("req", "ffn")),
        P("kvh", ("req", "ffn")),
        P(("req", "ffn"), "kvh"),
    )
    out_specs = P(("req", "ffn"), "kvh")
    return jax.shard_map(local, mesh=mesh, in_specs=in_specs, out_specs=out_specs, check_vma=False)
```

time: 563 us -> 336 us (0.60)
  waiting for transfers between devices: 417 us -> 15 us
  Pallas kernels: 0 us -> 214 us
  matrix products: 68.4 us -> 46.3 us
  other arithmetic: 17.4 us -> 2.7 us
  between operations: 14.3 us -> 0.79 us
  starting transfers between devices: 0.43 us -> 7.72 us
    pallas_call x0 -> x5, Pallas kernels: none -> 214 us  [the longest x2 78.2 us: gather_tokens(): pl.pallas_call(functools.partial(gather_body, dims=dims, pieces=pieces),...]
    reduce_scatter x3 -> x0, waiting for transfers between devices: 212 us -> none  [the longest x1 104 us: local(): lax.psum_scatter(jnp.dot(activation, down_weight, preferred_element_type=...]
    all_gather x4 -> x0, waiting for transfers between devices: 205 us -> none  [the longest x1 73.9 us: local(): lax.all_gather(attention, 'req', axis=0, tiled=True)]
    dot_general x15 -> x1, matrix products: 31.8 us -> 5.79 us  [local(): jnp.dot(gather_tokens(attention, 1), out_weight, preferred_element_type=j...]
    all_to_all x0 -> x2, waiting for transfers between devices: none -> 15 us  [the longest x1 15 us: local(): lax.all_to_all(regrouped, 'kvh', split_axis=1, concat_axis=0, tiled=True)]
    all_to_all x0 -> x2, starting transfers between devices: none -> 7.72 us  [the longest x1 4.23 us: local(): lax.all_to_all(regrouped, 'kvh', split_axis=1, concat_axis=0, tiled=True)]
    convert_element_type x3 -> x1, other arithmetic: 6.69 us -> 0.81 us  [local(): (state * lax.rsqrt(squares / features + EPSILON)[:, None] * norm_gain).as...]
  transfers between devices with their start and end apart: 7 -> 2, of which waited for: 7 -> 1; matrix products, arithmetic and copies ran while one was open for 0% -> 0% of each run, Pallas kernels for 0% -> 0%
where the time goes in v1:
time: 336 us; the launch traced here: 335 us
  Pallas kernels  214 us (64%)
  matrix products  46.3 us (14%)
  blocking collectives  38.3 us (11%)
  waiting for transfers between devices  15 us (4%)
  local copies, waits for them, and re-layouts  9.94 us (3%)
  starting transfers between devices  7.72 us (2%)
    pallas_call x2, Pallas kernels, gather_tokens(): pl.pallas_call(functools.partial(gather_body, dims=dims, pieces=pieces),...  78.2 us
    pallas_call x1, Pallas kernels, gated(): pl.pallas_call(functools.partial(gated_body, pieces=pieces), out_shape=ja...  66.8 us
    pallas_call x1, Pallas kernels, scatter_tokens(): pl.pallas_call(functools.partial(scatter_body, dims=dims, pieces=pieces),...  43.4 us
    all_to_all x1, blocking collectives, local(): lax.all_to_all(partial_rows, ('req', 'ffn'), split_axis=0, concat_axis=1,...  31 us
    pallas_call x1, Pallas kernels, attention_part(): pl.pallas_call(body, out_shape=(jax.ShapeDtypeStruct((nodes, width), jnp....  25.4 us
    all_to_all x1, waiting for transfers between devices, local(): lax.all_to_all(regrouped, 'kvh', split_axis=1, concat_axis=0, tiled=True)  15 us
    dot_general x1, matrix products, local(): up_part = jnp.dot(block_rows, up_weight, preferred_element_type=jnp.float32)  14.5 us
    dot_general x1, matrix products, local(): jnp.dot(activation, down_weight, preferred_element_type=jnp.float32)  13.6 us
  transfers between devices with their start and end apart: 2, of which 1 were waited for; matrix products, arithmetic and copies ran while one was open for 0% of the time, Pallas kernels for 0%

profile of v1, /device:TPU:0, one launch (start us, length us, event | category | flops | bytes accessed | tf_op | source)
XLA Modules:
  0.0 334.6 jit_solution(5801514663696892652)
XLA Ops:
  0.0 1.2 dynamic_slice.14
  1.9 0.6 pad_add_fusion.len_ref
  2.5 25.4 %shard_map.127 = (bf16[64,4096]{1,0:T(8,128)(2,1)}, f32[4,2,512]{2,1,0:T(2,128)}) custom-call(s32[2]{0:T(128)} %pad_add_fusion.len_ref, bf16[64,4096]{1,0:T(8,128)(2,1)} %bitcast.63, bf16[64,512]{1,0:T(8,128)(2,1)} %bitcast.66, bf16[64,512]{1,0:T(8,128)(2,1)} %bitcast.67, bf16[4,4096,128]{2,1,0:T(8,128)(2,1)} %bitcast.56, bf16[4,4096,128]{2,1,0:T(8,128)(2,1)} %bitcast.57, ...), custom_call_target="tpu_custom_call" | custom-call | tf_op jit(solution)/shard_map/pallas_call | solution.py:89
  27.9 3.5 %all-to-all-start = ((bf16[2,32,4096]{2,1,0:T(8,128)(2,1)}), bf16[2,32,4096]{2,1,0:T(8,128)(2,1)S(1)}, u32[]{:S(2)}, u32[]{:S(2)}) async-start(bf16[2,32,4096]{2,1,0:T(8,128)(2,1)} %bitcast.64), calls=%async_computation | async-start | bytes 1048576 | tf_op jit(solution)/shard_map/all_to_all | solution.py:447
  31.4 2.2 all-gather
  33.6 0.1 slice_reduce_fusion
  33.8 0.1 squeeze.43
  34.1 0.1 fusion.9
  34.3 0.3 mul.46
  34.6 0.2 mul.47
  34.8 0.8 multiply_reduce_fusion.x_ref
  35.6 39.4 %shard_map.128 = bf16[4,2,2,32,4096]{4,3,2,1,0:T(8,128)(2,1)} custom-call(bf16[32,4096]{1,0:T(8,128)(2,1)} %multiply_reduce_fusion.x_ref), custom_call_target="tpu_custom_call" | custom-call | tf_op jit(solution)/shard_map/pallas_call | solution.py:215
  75.1 5.8 %fusion.6 = f32[16,32,512]{2,1,0:T(8,128)S(1)} fusion(bf16[16,32,4096]{2,1,0:T(8,128)(2,1)} %bitcast.60, bf16[4096,512]{1,0:T(8,128)(2,1)} %param.21), kind=kOutput, calls=%fused_computation.6 | convolution fusion | flops 2147483648 | bytes 9437184 | tf_op jit(solution)/shard_map/dot_general | solution.py:454
  80.9 31.0 %all_to_all.35 = f32[16,32,512]{2,1,0:T(8,128)S(1)} all-to-all(f32[16,32,512]{2,1,0:T(8,128)S(1)} %fusion.6), channel_id=1, replica_groups=mesh['req'=8,'kvh'=2,'ffn'=2] {'req','ffn'}, dimensions={0} | all-to-all | bytes 2097152 | tf_op jit(solution)/shard_map/all_to_all | solution.py:455
  111.9 0.6 copy.21
  112.5 0.9 all_to_all.30
  113.4 1.6 copy.22
  115.1 4.2 %all-to-all-start.2 = ((f32[32,2,4096]{2,0,1:T(8,128)}), f32[32,2,4096]{2,0,1:T(8,128)S(1)}, u32[]{:S(2)}, u32[]{:S(2)}) async-start(f32[32,2,4096]{2,0,1:T(8,128)} %copy.22), calls=%async_computation.2 | async-start | bytes 2097152 | tf_op jit(solution)/shard_map/all_to_all | solution.py:458
  119.3 15.0 %all-to-all-done.2 = f32[32,2,4096]{2,0,1:T(8,128)S(1)} async-done(((f32[32,2,4096]{2,0,1:T(8,128)}), f32[32,2,4096]{2,0,1:T(8,128)S(1)}, u32[]{:S(2)}, u32[]{:S(2)}) %all-to-all-start.2) | async-done | bytes 1048608 | tf_op jit(solution)/shard_map/all_to_all | solution.py:458
  134.3 0.1 reduce_sum.38
  134.4 0.2 multiply_reduce_fusion.1
  134.6 5.1 %psum.7 = f32[32]{0:T(128)S(1)} all-reduce(f32[32]{0:T(128)S(1)} %get-tuple-element.11), channel_id=1, replica_groups=mesh['req'=8,'kvh'=2,'ffn'=2] {'kvh'}, use_global_device_ids=true, to_apply=%region_5.6 | all-reduce | flops 32 | bytes 256 | tf_op jit(solution)/shard_map/psum | solution.py:461
  139.7 0.8 multiply_convert_fusion.x_ref
  140.5 38.7 %shard_map.129 = bf16[4,2,2,32,4096]{4,3,2,1,0:T(8,128)(2,1)} custom-call(bf16[32,4096]{1,0:T(8,128)(2,1)} %multiply_convert_fusion.x_ref), custom_call_target="tpu_custom_call" | custom-call | tf_op jit(solution)/shard_map/pallas_call | solution.py:215
  179.3 14.5 %fusion.15 = (bf16[2,256,1792]{2,1,0:T(8,128)(2,1)}, f32[2,256,1792]{2,1,0:T(8,128)S(1)}) fusion(bf16[2,256,4096]{2,1,0:T(8,128)(2,1)} %bitcast.58, bf16[4096,1792]{1,0:T(8,128)(2,1)} %param.24), kind=kOutput, calls=%fused_computation.29 | convolution fusion | flops 7517110272 | bytes 24379392 | tf_op jit(solution)/shard_map/dot_general | solution.py:465
  193.7 12.5 %fusion.14 = (bf16[2,256,1792]{2,1,0:T(8,128)(2,1)}, f32[2,256,1792]{2,1,0:T(8,128)S(1)}) fusion(bf16[2,256,4096]{2,1,0:T(8,128)(2,1)S(1)} %bitcast.59, bf16[4096,1792]{1,0:T(8,128)(2,1)} %param.23), kind=kOutput, calls=%fused_computation.28 | convolution fusion | flops 7517110272 | bytes 24379392 | tf_op jit(solution)/shard_map/dot_general | solution.py:464
  206.2 1.3 dynamic-slice_bitcast_fusion.own_up_ref
  207.6 1.4 dynamic-slice_bitcast_fusion.1.own_gate_ref
  208.9 66.8 %shard_map.130 = bf16[2,256,1792]{2,1,0:T(8,128)(2,1)} custom-call(bf16[2,256,1792]{2,1,0:T(8,128)(2,1)} %get-tuple-element.15.gate_ref, bf16[2,256,1792]{2,1,0:T(8,128)(2,1)} %get-tuple-element.17.up_ref, f32[256,1792]{1,0:T(8,128)} %dynamic-slice_bitcast_fusion.1.own_gate_ref, f32[256,1792]{1,0:T(8,128)} %dynamic-slice_bitcast_fusion.own_up_ref), custom_call_target="tpu_custom_call" | custom-call | tf_op jit(solution)/shard_map/pallas_call | solution.py:400
  275.8 13.6 %fusion.x_ref = f32[4,2,2,32,4096]{4,3,2,1,0:T(8,128)} fusion(bf16[4,2,2,32,1792]{4,3,2,1,0:T(8,128)(2,1)} %bitcast.62, bf16[1792,4096]{1,0:T(8,128)(2,1)} %param.25), kind=kOutput, calls=%fused_computation | convolution fusion | flops 7516192768 | bytes 24903680 | tf_op jit(solution)/shard_map/dot_general | solution.py:467
  289.3 43.4 %shard_map.131 = f32[32,4096]{1,0:T(8,128)} custom-call(f32[4,2,2,32,4096]{4,3,2,1,0:T(8,128)} %fusion.x_ref, f32[32,4096]{1,0:T(8,128)} %copy-done), custom_call_target="tpu_custom_call" | custom-call | tf_op jit(solution)/shard_map/pallas_call | solution.py:317
  332.7 1.9 copy.29
  (17 shorter events, 0.4 us)
Async XLA Ops:
  27.9 6.9 %all-to-all-start = ((bf16[2,32,4096]{2,1,0:T(8,128)(2,1)}), bf16[2,32,4096]{2,1,0:T(8,128)(2,1)S(1)}, u32[]{:S(2)}, u32[]{:S(2)}) async-start(bf16[2,32,4096]{2,1,0:T(8,128)(2,1)} %bitcast.64), calls=%async_computation | async-start | bytes 1048576 | tf_op jit(solution)/shard_map/all_to_all | solution.py:447
  112.5 21.9 %copy-start.2 = (f32[32,4096]{1,0:T(8,128)S(1)}, f32[32,4096]{1,0:T(8,128)}, u32[]{:S(2)}) copy-start(f32[32,4096]{1,0:T(8,128)} %param.20) | copy-start | bytes 1572868
  113.4 26.3 %copy-start.3 = (f32[4096]{0:T(1024)S(1)}, f32[4096]{0:T(1024)}, u32[]{:S(2)}) copy-start(f32[4096]{0:T(1024)} %param.22) | copy-start | bytes 49156
  115.1 19.2 %all-to-all-start.2 = ((f32[32,2,4096]{2,0,1:T(8,128)}), f32[32,2,4096]{2,0,1:T(8,128)S(1)}, u32[]{:S(2)}, u32[]{:S(2)}) async-start(f32[32,2,4096]{2,0,1:T(8,128)} %copy.22), calls=%async_computation.2 | async-start | bytes 2097152 | tf_op jit(solution)/shard_map/all_to_all | solution.py:458
  134.6 59.1 %copy-start = (f32[32,4096]{1,0:T(8,128)}, f32[32,4096]{1,0:T(8,128)S(1)}, u32[]{:S(2)}) copy-start(f32[32,4096]{1,0:T(8,128)S(1)} %get-tuple-element.12.state_ref) | copy-start | bytes 1572868
  179.3 14.5 %copy-start.1 = (bf16[4,2,2,32,4096]{4,3,2,1,0:T(8,128)(2,1)S(1)}, bf16[4,2,2,32,4096]{4,3,2,1,0:T(8,128)(2,1)}, u32[]{:S(2)}) copy-start(bf16[4,2,2,32,4096]{4,3,2,1,0:T(8,128)(2,1)} %shard_map.129) | copy-start | bytes 12582916
